TPU v7x, 32 devices: a whole 2x2x4 slice. The times are simulated.
32 devices in a mesh: sp: 16 (over z, y, core), flt: 2 (over x).
Axes of the slice: x: 2, y: 2, z: 4, core: 2. Of those that a mesh axis runs over, the one named last changes fastest.
Arguments:
- activations: bfloat16 [32, 16, 8, 256], P('sp', 'flt'), may hold values from -6 to 6
- w_first: bfloat16 [256, 3, 3, 3, 256], P('flt'), may hold values from -0.078125 to 0.078125
- w_second: bfloat16 [256, 3, 3, 3, 256], P('flt'), may hold values from -0.078125 to 0.078125
- cotangent: bfloat16 [16, 8, 4, 256], P('sp', 'flt'), may hold values from -6 to 6
Outputs:
- section_out: float32 [16, 8, 4, 256], P('sp', 'flt')
- grad_input: float32 [32, 16, 8, 256], P('sp', 'flt')
- grad_first: float32 [256, 3, 3, 3, 256], P('flt')
- grad_second: float32 [256, 3, 3, 3, 256], P('flt')
All inputs are finite; a program needn't handle non-finite values.
Results may differ from a plain program's by a relative error of at most 0.0045.
Values may be sent and summed in bfloat16 or wider, within the bound.
A program may use at most 64 MiB of HBM per device.

v0:
```python
import jax
import jax.numpy as jnp
from jax import lax
from jax.sharding import PartitionSpec as P


def with_halo(cells, sides, width):
    for axis, dim in sides:
        count = lax.axis_size(axis)
        ends = count - 1
        head = lax.slice_in_dim(cells, 0, width, axis=dim)
        tail = lax.slice_in_dim(cells, cells.shape[dim] - width, cells.shape[dim], axis=dim)
        cells = jnp.concatenate(
            [
                lax.ppermute(tail, axis, [(i, (i + 1) % count) for i in range(ends)]),
                cells,
                lax.ppermute(head, axis, [((i + 1) % count, i) for i in range(ends)]),
            ],
            axis=dim,
        )
    return cells


def shifted(shard, axis, by):
    peers = lax.axis_size(axis)
    pairs = [(i, i + by) for i in range(peers) if 0 <= i + by < peers]
    return lax.ppermute(shard, axis, pairs)


def conv_plain(field, kernel, strides, pads, dilate):
    return lax.conv_general_dilated(
        field[None],
        kernel,
        strides,
        pads,
        lhs_dilation=dilate,
        dimension_numbers=("NDHWC", "DHWIO", "NDHWC"),
        preferred_element_type=jnp.float32,
    )[0]


def filter_grad(field, errors, dilate, pads):
    return lax.conv_general_dilated(
        field[None],
        errors[None],
        (1, 1, 1),
        pads,
        rhs_dilation=dilate,
        dimension_numbers=("CDHWN", "IDHWO", "CDHWN"),
        preferred_element_type=jnp.float32,
    )


def silu_slope(value):
    sig = jax.nn.sigmoid(value)
    return sig * (1.0 + value * (1.0 - sig))


def forward_taps(kernel):
    return jnp.transpose(kernel, (1, 2, 3, 4, 0))


def turned(kernel):
    return jnp.transpose(kernel[:, ::-1, ::-1, ::-1], (1, 2, 3, 0, 4))


def fold_rims(core, arrived):
    first = core[0:1] + arrived[0:1]
    last = core[-1:] + arrived[3:4]
    return jnp.concatenate([first, core[1:-1], last], 0)


def per_device(activations, w_first, w_second, cotangent):
    planes = activations.shape[0]
    single = (1, 1, 1)
    double = (2, 2, 2)
    padded = with_halo(activations, (("sp", 0),), 1)
    x_wide = lax.all_gather(padded, "flt", axis=1, tiled=True)
    first_pre = conv_plain(x_wide, forward_taps(w_first), single, ((0, 0), (1, 1), (1, 1)), single)
    hidden = jax.nn.silu(first_pre).astype(jnp.bfloat16)
    below = shifted(hidden[planes - 1 :], "sp", 1)
    h_wide = lax.all_gather(jnp.concatenate([below, hidden], 0), "flt", axis=3, tiled=True)
    second_pre = conv_plain(
        h_wide, forward_taps(w_second), double, ((0, 0), (1, 0), (1, 0)), single
    )
    section_part = jax.nn.silu(second_pre)
    section_out = lax.all_to_all(section_part, "flt", split_axis=1, concat_axis=3, tiled=True)
    cot_part = lax.all_to_all(cotangent, "flt", split_axis=3, concat_axis=1, tiled=True)
    second_err = (cot_part.astype(jnp.float32) * silu_slope(second_pre)).astype(jnp.bfloat16)
    grad_second_part = filter_grad(h_wide, second_err, double, ((0, 0), (1, 0), (1, 0)))
    back_hidden = conv_plain(second_err, turned(w_second), single, ((2, 2), (1, 2), (1, 2)), double)
    shares = lax.psum_scatter(back_hidden, "flt", scatter_dimension=3, tiled=True)
    from_above = shifted(shares[0:1], "sp", -1)
    hidden_err = jnp.concatenate([shares[1:planes], shares[planes:] + from_above], 0)
    first_err = (hidden_err * silu_slope(first_pre)).astype(jnp.bfloat16)
    grad_first_part = filter_grad(x_wide, first_err, single, ((0, 0), (1, 1), (1, 1)))
    back_input = conv_plain(first_err, turned(w_first), single, ((2, 2), (1, 1), (1, 1)), single)
    shares_in = lax.psum_scatter(back_input, "flt", scatter_dimension=1, tiled=True)
    rim_pair = jnp.concatenate([shares_in[0:1], shares_in[planes + 1 :]], 0)
    arrived = with_halo(rim_pair, (("sp", 0),), 1)
    grad_input = fold_rims(shares_in[1 : planes + 1], arrived)
    grad_first, grad_second = lax.psum((grad_first_part, grad_second_part), "sp")
    return (section_out, grad_input, grad_first, grad_second)


def solution(mesh):
    placed = (
        P("sp", "flt", None, None),
        P("flt", None, None, None, None),
        P("flt", None, None, None, None),
        P("sp", "flt", None, None),
    )
    return jax.shard_map(
        per_device,
        mesh=mesh,
        in_specs=placed,
        out_specs=(
            P("sp", "flt", None, None),
            P("sp", "flt", None, None),
            P("flt", None, None, None, None),
            P("flt", None, None, None, None),
        ),
        check_vma=False,
    )
```

profile of v0, /device:TPU:0, one launch (start us, length us, event | category | flops | bytes accessed | tf_op | source)
XLA Modules:
  0.0 260.4 jit_solution(1050959158090861135)
XLA Ops:
  7.2 0.0 copy-start
  7.2 0.0 reduce-scatter.6.cloned.1.call-start
  7.2 0.9 fusion.21
  8.1 2.4 collective-permute-start
  10.5 1.3 collective-permute-start.1
  11.8 0.0 collective-permute-done
  11.8 3.9 %collective-permute-done.1 = bf16[1,8,8,256]{3,2,1,0:T(8,128)(2,1)S(1)} collective-permute-done((bf16[1,8,8,256]{3,2,1,0:T(8,128)(2,1)S(1)}, bf16[1,8,8,256]{3,2,1,0:T(8,128)(2,1)S(1)}, u32[]{:S(2)}, u32[]{:S(2)}) %collective-permute-start.1) | collective-permute-done | bytes 32800 | tf_op jit(solution)/shard_map/ppermute | solution.py:17
  15.7 0.9 pad_maximum_fusion
  16.6 5.6 %all_gather.6 = bf16[4,16,8,256]{3,2,1,0:T(8,128)(2,1)S(1)} all-gather(bf16[4,8,8,256]{3,2,1,0:T(8,128)(2,1)S(1)} %pad_maximum_fusion), channel_id=1, replica_groups=mesh['sp'=16,'flt'=2] {'flt'}, dimensions={1}, use_global_device_ids=true | all-gather | bytes 393216 | tf_op jit(solution)/shard_map/all_gather | solution.py:78
  22.2 0.0 copy-done
  22.2 0.0 copy-start.1
  22.2 2.9 %fusion.2 = f32[1,2,16,8,128]{4,0,3,2,1:T(1,128)S(1)} fusion(bf16[128,3,3,3,256]{4,0,3,2,1:T(8,128)(2,1)S(1)} %copy-done, bf16[1,4,16,8,256]{4,3,2,1,0:T(8,128)(2,1)S(1)} %bitcast.77), kind=kOutput, calls=%fused_computation.2 | convolution fusion | flops 397934592 | bytes 2162688 | tf_op jit(solution)/shard_map/conv_general_dilated | solution.py:31
  25.2 3.4 %collective-permute-start.2 = (bf16[1,16,8,128]{3,2,1,0:T(8,128)(2,1)S(1)}, bf16[1,16,8,128]{3,2,1,0:T(8,128)(2,1)S(1)}, u32[]{:S(2)}, u32[]{:S(2)}) collective-permute-start(bf16[1,16,8,128]{3,2,1,0:T(8,128)(2,1)S(1)} %slice.43), channel_id=1, source_target_pairs={{0,2},{2,4},{4,6},{6,8},{8,10},{10,12},{12,14},{14,16},{16,18},{18... | collective-permute-start | bytes 98312 | tf_op jit(solution)/shard_map/ppermute | solution.py:27
  28.6 0.0 copy-done.1
  28.6 0.2 copy.40
  28.8 0.3 reshape.76
  29.1 6.4 %all_to_all.27 = bf16[2,2,1024]{2,1,0:T(2,128)(2,1)S(1)} all-to-all(bf16[2,2,1024]{2,1,0:T(2,128)(2,1)S(1)} %reshape.76), channel_id=1, replica_groups=mesh['sp'=16,'flt'=2] {'flt'}, dimensions={0} | all-to-all | bytes 16384 | tf_op jit(solution)/shard_map/all_to_all | solution.py:88
  35.5 0.6 reshape.77
  36.1 0.2 copy.41
  36.2 0.0 collective-permute-done.2
  36.3 5.5 %all_gather.7 = bf16[3,16,8,256]{3,2,1,0:T(8,128)(2,1)S(1)} all-gather(bf16[3,16,8,128]{3,2,1,0:T(8,128)(2,1)S(1)} %pad_maximum_fusion.2), channel_id=1, replica_groups=mesh['sp'=16,'flt'=2] {'flt'}, dimensions={3}, use_global_device_ids=true | all-gather | bytes 294912 | tf_op jit(solution)/shard_map/all_gather | solution.py:82
  41.8 0.0 copy-start.2
  41.8 2.5 fusion.6
  44.3 0.0 copy-done.2
  44.3 1.7 fusion.19
  46.0 0.8 copy.77
  46.8 0.0 reduce-scatter.6.cloned.1.call-update
  46.8 0.0 reduce-scatter.8.cloned.1.call-start
  46.9 14.3 %reduce-scatter.6.cloned.1.call-done = f32[3,16,8,128]{3,2,1,0:T(8,128)} async-done(((f32[3,16,8,256]{3,2,1,0:T(8,128)}), f32[3,16,8,128]{3,2,1,0:T(8,128)}) %reduce-scatter.6.cloned.1.call-update) | async-done | bytes 196624 | tf_op jit(solution)/shard_map/reduce_scatter | solution.py:92
  61.2 0.9 slice_bitcast_fusion.4
  62.1 1.5 collective-permute-start.3
  63.5 2.9 %fusion.4 = f32[128,3,3,3,256]{0,4,3,2,1:T(8,128)} fusion(bf16[1,3,16,8,256]{4,3,2,1,0:T(8,128)(2,1)S(1)} %bitcast.81, f32[1,1,8,4,128]{4,0,3,2,1:T(1,128)S(1)} %bitcast.84, f32[1,1,8,4,128]{4,0,3,2,1:T(1,128)S(1)} %fusion.6), kind=kOutput, calls=%fused_computation.5 | convolution fusion | flops 49778688 | bytes 3768320 | tf_op jit(solution)/shard_map/conv_general_dilated | solution.py:43
  66.4 0.0 collective-permute-done.3
  66.4 0.8 fusion.14
  67.3 0.1 fusion.8
  67.4 4.5 %fusion.10 = f32[1,4,16,8,256]{4,0,3,2,1:T(1,128)S(1)} fusion(bf16[128,3,3,3,256]{4,0,3,2,1:T(8,128)(2,1)S(1)} %copy-done, bf16[1,2,16,8,128]{4,3,2,1,0:T(8,128)(2,1)S(1)} %fusion.8), kind=kOutput, calls=%fused_computation.16 | convolution fusion | flops 397934592 | bytes 2359296 | tf_op jit(solution)/shard_map/conv_general_dilated | solution.py:31
  72.0 1.1 copy.59
  73.0 0.0 reduce-scatter.8.cloned.1.call-update
  73.1 0.0 all-reduce.3.cloned.1.call-start
  73.1 5.6 %fusion = f32[128,3,3,3,256]{0,4,3,2,1:T(8,128)} fusion(bf16[1,4,16,8,256]{4,3,2,1,0:T(8,128)(2,1)S(1)} %bitcast.78, bf16[1,2,16,8,128]{4,3,2,1,0:T(8,128)(2,1)S(1)} %fusion.8), kind=kOutput, calls=%fused_computation | convolution fusion | flops 397934592 | bytes 3866624 | tf_op jit(solution)/shard_map/conv_general_dilated | solution.py:43
  78.7 0.0 all-reduce.3.cloned.1.call-update
  78.8 9.9 %reduce-scatter.8.cloned.1.call-done = f32[8,8192]{1,0:T(8,128)} async-done(((f32[16,8192]{1,0:T(8,128)}), f32[8,8192]{1,0:T(8,128)}) %reduce-scatter.8.cloned.1.call-update) | async-done | bytes 262160
  88.6 1.0 copy.78
  89.7 1.6 collective-permute-start.4
  91.3 1.3 collective-permute-start.5
  92.6 6.2 %all_to_all.28 = f32[1,8,4,128]{3,2,0,1:T(4,128)S(1)} all-to-all(f32[1,8,4,128]{3,2,0,1:T(4,128)S(1)} %copy.38), channel_id=1, replica_groups=mesh['sp'=16,'flt'=2] {'flt'}, dimensions={1} | all-to-all | bytes 32768 | tf_op jit(solution)/shard_map/all_to_all | solution.py:87
  98.8 0.6 copy.79
  99.4 0.0 collective-permute-done.4
  99.4 0.0 collective-permute-done.5
  99.4 0.7 pad_maximum_fusion.1
  100.1 143.5 %all-reduce.3.cloned.1.call-done = (f32[128,3,3,3,256]{0,4,3,2,1:T(8,128)}, f32[128,3,3,3,256]{0,4,3,2,1:T(8,128)}) async-done(((f32[128,3,3,3,256]{0,4,3,2,1:T(8,128)}, f32[128,3,3,3,256]{0,4,3,2,1:T(8,128)}), (f32[128,3,3,3,256]{0,4,3,2,1:T(8,128)}, f32[128,3,3,3,256]{0,4,3,2,1:T(8,128)})) %all-reduce.3.cloned.1.call-update) | async-done | bytes 7077904 | tf_op jit(solution)/shard_map/psum | solution.py:102
  243.6 5.2 %copy.48 = f32[128,3,3,3,256]{4,0,3,2,1:T(8,128)} copy(f32[128,3,3,3,256]{0,4,3,2,1:T(8,128)} %get-tuple-element.20) | data formatting | bytes 7077888
  248.7 5.2 %copy.49 = f32[128,3,3,3,256]{4,0,3,2,1:T(8,128)} copy(f32[128,3,3,3,256]{0,4,3,2,1:T(8,128)} %get-tuple-element.21) | data formatting | bytes 7077888
  (8 shorter events, 0.2 us)
Async XLA Ops:
  7.2 15.1 %copy-start = (bf16[128,3,3,3,256]{4,0,3,2,1:T(8,128)(2,1)S(1)}, bf16[128,3,3,3,256]{4,0,3,2,1:T(8,128)(2,1)}, u32[]{:S(2)}) copy-start(bf16[128,3,3,3,256]{4,0,3,2,1:T(8,128)(2,1)} %param.5) | copy-start | bytes 5308420
  7.2 54.0 %reduce-scatter.6.cloned.1.call-start = ((), (), s32[]{:S(2)}) async-start(), calls=%async_computation.4 | async-start | bytes 589824 | tf_op jit(solution)/shard_map/reduce_scatter | solution.py:92
  8.1 3.7 %collective-permute-start = (bf16[1,8,8,256]{3,2,1,0:T(8,128)(2,1)S(1)}, bf16[1,8,8,256]{3,2,1,0:T(8,128)(2,1)S(1)}, u32[]{:S(2)}, u32[]{:S(2)}) collective-permute-start(bf16[1,8,8,256]{3,2,1,0:T(8,128)(2,1)S(1)} %get-tuple-element.28), channel_id=1, source_target_pairs={{0,2},{2,4},{4,6},{6,8},{8,10},{10,12},{12,14},{14,16},{16,18},{18... | collective-permute-start | bytes 98312 | tf_op jit(solution)/shard_map/ppermute | solution.py:15
  10.5 5.2 %collective-permute-start.1 = (bf16[1,8,8,256]{3,2,1,0:T(8,128)(2,1)S(1)}, bf16[1,8,8,256]{3,2,1,0:T(8,128)(2,1)S(1)}, u32[]{:S(2)}, u32[]{:S(2)}) collective-permute-start(bf16[1,8,8,256]{3,2,1,0:T(8,128)(2,1)S(1)} %get-tuple-element.29), channel_id=1, source_target_pairs={{2,0},{4,2},{6,4},{8,6},{10,8},{12,10},{14,12},{16,14},{18,16},{20... | collective-permute-start | bytes 98312 | tf_op jit(solution)/shard_map/ppermute | solution.py:17
  22.2 6.3 %copy-start.1 = (bf16[1,4,4,256]{3,2,1,0:T(4,128)(2,1)S(1)}, bf16[1,4,4,256]{3,2,1,0:T(4,128)(2,1)}, u32[]{:S(2)}) copy-start(bf16[1,4,4,256]{3,2,1,0:T(4,128)(2,1)} %param.7) | copy-start | bytes 24580
  25.2 11.1 %collective-permute-start.2 = (bf16[1,16,8,128]{3,2,1,0:T(8,128)(2,1)S(1)}, bf16[1,16,8,128]{3,2,1,0:T(8,128)(2,1)S(1)}, u32[]{:S(2)}, u32[]{:S(2)}) collective-permute-start(bf16[1,16,8,128]{3,2,1,0:T(8,128)(2,1)S(1)} %slice.43), channel_id=1, source_target_pairs={{0,2},{2,4},{4,6},{6,8},{8,10},{10,12},{12,14},{14,16},{16,18},{18... | collective-permute-start | bytes 98312 | tf_op jit(solution)/shard_map/ppermute | solution.py:27
  41.8 2.5 copy-start.2
  46.8 41.8 %reduce-scatter.8.cloned.1.call-start = ((), (), s32[]{:S(2)}) async-start(), calls=%async_computation.5 | async-start | bytes 786432
  62.1 4.4 %collective-permute-start.3 = (f32[1,16,8,128]{3,2,1,0:T(8,128)S(1)}, f32[1,16,8,128]{3,2,1,0:T(8,128)S(1)}, u32[]{:S(2)}, u32[]{:S(2)}) collective-permute-start(f32[1,16,8,128]{3,2,1,0:T(8,128)S(1)} %get-tuple-element.27), channel_id=1, source_target_pairs={{2,0},{4,2},{6,4},{8,6},{10,8},{12,10},{14,12},{16,14},{18,16},{20... | collective-permute-start | bytes 196616 | tf_op jit(solution)/shard_map/ppermute | solution.py:27
  73.1 170.5 %all-reduce.3.cloned.1.call-start = ((), (), s32[]{:S(2)}) async-start(), calls=%async_computation.6 | async-start | bytes 14155776 | tf_op jit(solution)/shard_map/psum | solution.py:102
  89.7 9.7 %collective-permute-start.4 = (f32[1,8,8,256]{3,2,1,0:T(8,128)S(1)}, f32[1,8,8,256]{3,2,1,0:T(8,128)S(1)}, u32[]{:S(2)}, u32[]{:S(2)}) collective-permute-start(f32[1,8,8,256]{3,2,1,0:T(8,128)S(1)} %get-tuple-element.24), channel_id=1, source_target_pairs={{0,2},{2,4},{4,6},{6,8},{8,10},{10,12},{12,14},{14,16},{16,18},{18... | collective-permute-start | bytes 196616 | tf_op jit(solution)/shard_map/ppermute | solution.py:15
  91.3 8.2 %collective-permute-start.5 = (f32[1,8,8,256]{3,2,1,0:T(8,128)S(1)}, f32[1,8,8,256]{3,2,1,0:T(8,128)S(1)}, u32[]{:S(2)}, u32[]{:S(2)}) collective-permute-start(f32[1,8,8,256]{3,2,1,0:T(8,128)S(1)} %get-tuple-element.25), channel_id=1, source_target_pairs={{2,0},{4,2},{6,4},{8,6},{10,8},{12,10},{14,12},{16,14},{18,16},{20... | collective-permute-start | bytes 196616 | tf_op jit(solution)/shard_map/ppermute | solution.py:17
Sparse Core Ops, SparseCore 0:
  46.9 14.1 reduce-scatter.5
  73.2 15.3 reduce-scatter.7
  92.9 150.6 all-reduce.2
where the time goes:
time: 261 us; the launch traced here: 260 us
  waiting for transfers between devices  172 us (66%)
  blocking collectives  23.7 us (9%)
  matrix products  20.1 us (8%)
  local copies, waits for them, and re-layouts  17 us (7%)
  between operations  13.9 us (5%)
  starting transfers between devices  11.5 us (4%)
    psum x1, waiting for transfers between devices, per_device(): lax.psum((grad_first_part, grad_second_part), 'sp')  143 us
    unnamed x16, local copies, waits for them, and re-layouts  14.4 us
    reduce_scatter x1, waiting for transfers between devices, per_device(): lax.psum_scatter(back_hidden, 'flt', scatter_dimension=3, tiled=True)  14.3 us
    conv_general_dilated x4, matrix products, conv_plain(): lax.conv_general_dilated(field[None], kernel, strides, pads, lhs_dilation...  11.6 us
    unnamed x4, waiting for transfers between devices  9.92 us
    conv_general_dilated x2, matrix products, filter_grad(): lax.conv_general_dilated(field[None], errors[None], (1, 1, 1), pads, rhs_...  8.52 us
    all_to_all x1, blocking collectives, per_device(): lax.all_to_all(cotangent, 'flt', split_axis=3, concat_axis=1, tiled=True)  6.38 us
    all_to_all x1, blocking collectives, per_device(): lax.all_to_all(section_part, 'flt', split_axis=1, concat_axis=3, tiled=True)  6.2 us
  transfers between devices with their start and end apart: 9, of which 4 were waited for; matrix products, arithmetic and copies ran while one was open for 5% of the time, Pallas kernels for 0%

commit v1 on v0

v1 whole, which is shorter than its diff:
```python
import functools

import jax
import jax.numpy as jnp
from jax import lax
from jax.experimental import pallas as pl
from jax.experimental.pallas import tpu as pltpu
from jax.sharding import PartitionSpec as P

MESH = pl.DeviceIdType.MESH
VMEM = pl.BlockSpec(memory_space=pltpu.VMEM)
ROOM = 62 * 1024 * 1024


def remote(src, dst, send, recv, place):
    return pltpu.make_async_remote_copy(
        src_ref=src, dst_ref=dst, send_sem=send, recv_sem=recv, device_id=place, device_id_type=MESH
    )


def greet(places):
    barrier = pltpu.get_barrier_semaphore()
    for place in places:
        pl.semaphore_signal(barrier, inc=1, device_id=place, device_id_type=MESH)
    pl.semaphore_wait(barrier, len(places))


def line_kernel(count, own, out, local, recv, send_z, send_y, send_c):
    here, other = lax.axis_index("sp"), lax.axis_index("flt")
    deep = count // 4
    z, y, core = here // 4, (here // 2) % 2, here % 2

    def spot(zz, yy, cc):
        return (zz * 2 + yy) * 2 + cc

    far = [lax.rem(z + step, deep) for step in range(1, deep)]
    to_y = (spot(z, 1 - y, core), other)
    to_c = (spot(z, y, 1 - core), other)
    greet([(spot(zz, y, core), other) for zz in far] + [to_y, to_c])
    sends = []

    def push(src, slot, send, place):
        copy = remote(src, out.at[slot], send, recv.at[slot], place)
        copy.start()
        sends.append(copy)

    def arrived(slot):
        remote(own, out.at[slot], send_y.at[0], recv.at[slot], to_y).wait_recv()

    for n, zz in enumerate(far):
        push(own, here, send_z.at[n], (spot(zz, y, core), other))
    push(own, here, send_y.at[0], to_y)
    push(own, here, send_c.at[0], to_c)
    keep = pltpu.make_async_copy(own, out.at[here], local)
    keep.start()
    for n in range(1, deep):
        slot = spot(lax.rem(z + deep - n, deep), y, core)
        arrived(slot)
        push(out.at[slot], slot, send_y.at[n], to_y)
        push(out.at[slot], slot, send_c.at[n], to_c)
    for n in range(deep):
        slot = spot(lax.rem(z + deep - n, deep), 1 - y, core)
        arrived(slot)
        push(out.at[slot], slot, send_c.at[deep + n], to_c)
    for n in range(deep):
        for yy in (y, 1 - y):
            arrived(spot(lax.rem(z + deep - n, deep), yy, 1 - core))
    keep.wait()
    for copy in sends:
        copy.wait_send()


def gather_line(block, number):
    count = lax.axis_size("sp")
    deep = count // 4
    dma = pltpu.SemaphoreType.DMA
    return pl.pallas_call(
        functools.partial(line_kernel, count),
        out_shape=jax.ShapeDtypeStruct((count,) + block.shape, block.dtype),
        in_specs=[VMEM],
        out_specs=VMEM,
        scratch_shapes=[dma, dma((count,)), dma((max(deep - 1, 1),)), dma((deep,)), dma((2 * deep,))],
        compiler_params=pltpu.CompilerParams(
            collective_id=number, has_side_effects=True, vmem_limit_bytes=ROOM
        ),
    )(block)


def swap_kernel(count, split, *refs):
    kinds = len(split)
    ins, outs = refs[:kinds], refs[kinds : 2 * kinds]
    local, send, recv = refs[2 * kinds :]
    here, me = lax.axis_index("sp"), lax.axis_index("flt")
    peers = [lax.rem(me + step, count) for step in range(1, count)]
    greet([(here, peer) for peer in peers])
    sends, keeps = [], []
    for k in range(kinds):
        for n, peer in enumerate(peers):
            src = ins[k].at[peer] if split[k] else ins[k]
            copy = remote(src, outs[k].at[me], send.at[k, n], recv.at[k, me], (here, peer))
            copy.start()
            sends.append(copy)
        keep = pltpu.make_async_copy(ins[k].at[me] if split[k] else ins[k], outs[k].at[me], local.at[k])
        keep.start()
        keeps.append(keep)
    for k in range(kinds):
        for n, peer in enumerate(peers):
            src = ins[k].at[peer] if split[k] else ins[k]
            remote(src, outs[k].at[peer], send.at[k, n], recv.at[k, peer], (here, peer)).wait_recv()
    for copy in sends:
        copy.wait_send()
    for keep in keeps:
        keep.wait()


def swap(number, *pieces):
    count = lax.axis_size("flt")
    split = tuple(cut for _, cut in pieces)
    arrays = [array for array, _ in pieces]
    dma = pltpu.SemaphoreType.DMA
    shapes = [a.shape if cut else (count,) + a.shape for a, cut in pieces]
    return pl.pallas_call(
        functools.partial(swap_kernel, count, split),
        out_shape=[jax.ShapeDtypeStruct(s, a.dtype) for s, a in zip(shapes, arrays)],
        in_specs=[VMEM] * len(arrays),
        out_specs=[VMEM] * len(arrays),
        scratch_shapes=[
            dma((len(arrays),)),
            dma((len(arrays), max(count - 1, 1))),
            dma((len(arrays), count)),
        ],
        compiler_params=pltpu.CompilerParams(
            collective_id=number, has_side_effects=True, vmem_limit_bytes=ROOM
        ),
    )(*arrays)


def first_kernel(high, wide, x_ref, e_ref, out_ref, moved):
    planes, flat, outs = e_ref.shape
    lane = lax.broadcasted_iota(jnp.int32, (outs, flat), 1)
    row, col = lane // wide, lane % wide
    blank = jnp.zeros((9 * outs, flat), jnp.bfloat16)
    moved[:, 0:flat] = blank
    moved[:, (planes + 1) * flat : (planes + 2) * flat] = blank

    def fill(plane, carry):
        errors = jnp.transpose(e_ref[plane].astype(jnp.float32))
        start = pl.multiple_of((plane + 1) * flat, flat)
        for ky in range(3):
            for kz in range(3):
                by = (ky - 1) * wide + (kz - 1)
                there_y, there_z = row - (ky - 1), col - (kz - 1)
                inside = (there_y >= 0) & (there_y < high) & (there_z >= 0) & (there_z < wide)
                turned_by = pltpu.roll(errors, by % flat, 1) if by else errors
                at = (ky * 3 + kz) * outs
                moved[at : at + outs, pl.ds(start, flat)] = jnp.where(inside, turned_by, 0.0).astype(
                    jnp.bfloat16
                )
        return carry

    lax.fori_loop(0, planes, fill, 0)

    def tap(step, carry):
        kx, ky = step // 3, step % 3
        left = moved[
            pl.ds(pl.multiple_of(ky * 3 * outs, 3 * outs), 3 * outs),
            pl.ds(pl.multiple_of((2 - kx) * flat, flat), planes * flat),
        ]
        out_ref[step] = jnp.dot(left, x_ref[...], preferred_element_type=jnp.float32)
        return carry

    lax.fori_loop(0, 9, tap, 0)


def first_grad(x_cells, errors, high, wide):
    planes, flat, outs = errors.shape
    ins = x_cells.shape[1]
    found = pl.pallas_call(
        functools.partial(first_kernel, high, wide),
        out_shape=jax.ShapeDtypeStruct((9, 3 * outs, ins), jnp.float32),
        in_specs=[VMEM, VMEM],
        out_specs=VMEM,
        scratch_shapes=[pltpu.VMEM((9 * outs, (planes + 2) * flat), jnp.bfloat16)],
        compiler_params=pltpu.CompilerParams(vmem_limit_bytes=ROOM),
        cost_estimate=pl.CostEstimate(
            flops=54 * outs * ins * planes * flat, bytes_accessed=8 * planes * flat * ins, transcendentals=0
        ),
    )(x_cells, errors)
    return jnp.transpose(found.reshape(3, 3, 3, outs, ins), (3, 0, 1, 2, 4))


def second_kernel(high, wide, h_ref, e_ref, out_ref):
    rows, _, flat, ins = h_ref.shape
    cells, outs = e_ref.shape
    errors = jnp.transpose(e_ref[...].astype(jnp.float32))
    lane = lax.broadcasted_iota(jnp.int32, (outs, cells), 1)
    col, line, deep = lane % wide, (lane // wide) % high, lane // flat
    found = {}
    for a in range(2):
        for b in range(2):
            for c in range(2):
                by = a * flat + b * wide + c
                ok = (deep + a < rows) & (line + b < high) & (col + c < wide)
                rolled = pltpu.roll(errors, (cells - by) % cells, 1) if by else errors
                found[a, b, c] = jnp.where(ok, rolled, 0.0).astype(jnp.bfloat16)
    for kx in range(3):
        for ky in range(3):
            for kz in range(3):
                kind = ((kx + 1) % 2 * 2 + (ky + 1) % 2) * 2 + (kz + 1) % 2
                left = found[int(kx == 0), int(ky == 0), int(kz == 0)]
                right = h_ref[:, kind].reshape(cells, ins)
                out_ref[(kx * 3 + ky) * 3 + kz] = jnp.dot(
                    left, right, preferred_element_type=jnp.float32
                )


def second_grad(hidden, errors, high, wide):
    rows, _, flat, ins = hidden.shape
    cells, outs = errors.shape
    found = pl.pallas_call(
        functools.partial(second_kernel, high, wide),
        out_shape=jax.ShapeDtypeStruct((27, outs, ins), jnp.float32),
        in_specs=[VMEM, VMEM],
        out_specs=VMEM,
        compiler_params=pltpu.CompilerParams(vmem_limit_bytes=ROOM),
        cost_estimate=pl.CostEstimate(
            flops=54 * outs * ins * cells, bytes_accessed=32 * cells * ins, transcendentals=0
        ),
    )(hidden, errors)
    return jnp.transpose(found.reshape(3, 3, 3, outs, ins), (3, 0, 1, 2, 4))


def shifted(shard, by):
    peers = lax.axis_size("sp")
    pairs = [(i, i + by) for i in range(peers) if 0 <= i + by < peers]
    return lax.ppermute(shard, "sp", pairs)


def conv_plain(field, kernel, strides, pads, dilate):
    return lax.conv_general_dilated(
        field[None],
        kernel,
        strides,
        pads,
        lhs_dilation=dilate,
        dimension_numbers=("NDHWC", "DHWIO", "NDHWC"),
        preferred_element_type=jnp.float32,
    )[0]


def silu_slope(value):
    sig = jax.nn.sigmoid(value)
    return sig * (1.0 + value * (1.0 - sig))


def forward_taps(kernel):
    return jnp.transpose(kernel, (1, 2, 3, 4, 0))


def turned(kernel):
    return jnp.transpose(kernel[:, ::-1, ::-1, ::-1], (1, 2, 3, 0, 4))


def window(whole, below, above, start, size):
    padded = jnp.pad(whole, ((below, above),) + ((0, 0),) * (whole.ndim - 1))
    return lax.dynamic_slice_in_dim(padded, start, size, 0)


def cut_last(array, count):
    parts = array.reshape(array.shape[:-1] + (count, array.shape[-1] // count))
    return jnp.moveaxis(parts, -2, 0)


def cut_rows(array, count):
    parts = array.reshape((array.shape[0], count, array.shape[1] // count) + array.shape[2:])
    return jnp.moveaxis(parts, 1, 0)


def join_rows(parts):
    moved = jnp.moveaxis(parts, 0, 1)
    return moved.reshape((moved.shape[0], moved.shape[1] * moved.shape[2]) + moved.shape[3:])


def join_last(parts):
    moved = jnp.moveaxis(parts, 0, -2)
    return moved.reshape(moved.shape[:-2] + (moved.shape[-2] * moved.shape[-1],))


def own_term(parts_f32, parts_sent, me):
    mine = lax.broadcasted_iota(jnp.int32, (parts_sent.shape[0],) + (1,) * (parts_sent.ndim - 1), 0) == me
    rest = jnp.sum(jnp.where(mine, 0.0, parts_sent.astype(jnp.float32)), 0)
    return rest + lax.dynamic_index_in_dim(parts_f32, me, 0, keepdims=False)


def per_device(activations, w_first, w_second, cotangent):
    planes = activations.shape[0]
    rows = cotangent.shape[0]
    place, me = lax.axis_index("sp"), lax.axis_index("flt")
    count = lax.axis_size("flt")
    line = lax.axis_size("sp")
    single = (1, 1, 1)
    double = (2, 2, 2)
    x_parts, cot_parts = swap(1, (activations, False), (cut_last(cotangent, count), True))
    x_wide, cot_part = join_rows(x_parts), join_rows(cot_parts)
    high, wide = x_wide.shape[1], x_wide.shape[2]
    ins = x_wide.shape[3]
    x_full = lax.all_gather(x_wide, "sp", axis=0, tiled=True)
    x_near = jnp.concatenate([shifted(x_wide, 1), x_wide, shifted(x_wide[:1], -1)], 0)
    first_pre = conv_plain(x_near, forward_taps(w_first), single, ((0, 0), (1, 1), (1, 1)), single)
    plane = lax.broadcasted_iota(jnp.int32, (planes + 1, 1, 1, 1), 0) + place * planes
    hidden = jnp.where(plane > 0, jax.nn.silu(first_pre), 0.0).astype(jnp.bfloat16)
    (h_parts,) = swap(2, (hidden, False))
    h_wide = join_last(h_parts)
    h_own = h_wide[1:].reshape(rows, 2, high // 2, 2, wide // 2, 2, ins)
    h_own = jnp.transpose(h_own, (0, 1, 3, 5, 2, 4, 6)).reshape(rows, 8, high * wide // 4, ins)
    h_full = lax.all_gather(h_own, "sp", axis=0, tiled=True)
    second_pre = conv_plain(
        h_wide, forward_taps(w_second), double, ((0, 0), (1, 0), (1, 0)), single
    )
    second_err = (cot_part.astype(jnp.float32) * silu_slope(second_pre)).astype(jnp.bfloat16)
    outs = second_err.shape[-1]
    e_full = gather_line(second_err.reshape(-1, outs), 3).reshape((line * rows,) + second_err.shape[1:])
    e_near = window(e_full, 0, 1, place * rows, rows + 1)
    back_hidden = conv_plain(e_near, turned(w_second), single, ((1, 0), (1, 2), (1, 2)), double)
    back_parts = cut_last(back_hidden, count)
    section_parts = cut_rows(jax.nn.silu(second_pre), count)
    got, section_got = swap(4, (back_parts.astype(jnp.bfloat16), True), (section_parts, True))
    section_out = join_last(section_got)
    hidden_err = own_term(back_parts, got, me)
    first_err = (hidden_err * silu_slope(first_pre[1:])).astype(jnp.bfloat16)
    f_full = gather_line(first_err.reshape(planes, high * wide, outs), 5)
    f_full = f_full.reshape(line * planes, high * wide, outs)
    f_near = window(f_full, 1, 1, place * planes, planes + 2).reshape(planes + 2, high, wide, outs)
    back_input = conv_plain(f_near, turned(w_first), single, ((0, 0), (1, 1), (1, 1)), single)
    in_parts = cut_rows(back_input, count)
    (in_got,) = swap(6, (in_parts.astype(jnp.bfloat16), True))
    grad_input = own_term(in_parts, in_got, me)
    grad_second = second_grad(h_full, e_full.reshape(-1, outs), high // 2, wide // 2)
    grad_first = first_grad(x_full.reshape(-1, ins), f_full, high, wide)
    return (section_out, grad_input, grad_first, grad_second)


def solution(mesh):
    placed = (
        P("sp", "flt", None, None),
        P("flt", None, None, None, None),
        P("flt", None, None, None, None),
        P("sp", "flt", None, None),
    )
    return jax.shard_map(
        per_device,
        mesh=mesh,
        in_specs=placed,
        out_specs=(
            P("sp", "flt", None, None),
            P("sp", "flt", None, None),
            P("flt", None, None, None, None),
            P("flt", None, None, None, None),
        ),
        check_vma=False,
    )
```

time: 261 us -> 135 us (0.52)
  waiting for transfers between devices: 172 us -> 4.15 us
  Pallas kernels: 0 us -> 82.4 us
  blocking collectives: 23.7 us -> 0 us
  starting transfers between devices: 11.5 us -> 2.66 us
  matrix products: 20.1 us -> 11.5 us
  local copies, waits for them, and re-layouts: 17 us -> 11.7 us
  other arithmetic: 2.53 us -> 7.73 us
    psum x1 -> x0, waiting for transfers between devices: 143 us -> none  [per_device(): lax.psum((grad_first_part, grad_second_part), 'sp')]
    pallas_call x0 -> x8, Pallas kernels: none -> 82.4 us  [the longest x2 32.4 us: gather_line(): pl.pallas_call(functools.partial(line_kernel, count), out_shape=jax.Shape...]
    reduce_scatter x1 -> x0, waiting for transfers between devices: 14.3 us -> none  [per_device(): lax.psum_scatter(back_hidden, 'flt', scatter_dimension=3, tiled=True)]
    unnamed x16 -> x11, local copies, waits for them, and re-layouts: 14.4 us -> 0.64 us
    all_to_all x2 -> x0, blocking collectives: 12.6 us -> none  [the longest x1 6.38 us: per_device(): lax.all_to_all(cotangent, 'flt', split_axis=3, concat_axis=1, tiled=True)]
    all_gather x2 -> x0, blocking collectives: 11.1 us -> none  [the longest x1 5.64 us: per_device(): x_wide = lax.all_gather(padded, 'flt', axis=1, tiled=True)]
    unnamed x4 -> x2, waiting for transfers between devices: 9.92 us -> 0.03 us
    ppermute x6 -> x2, starting transfers between devices: 11.4 us -> 2.58 us  [shifted(): return lax.ppermute(shard, 'sp', pairs)]
  transfers between devices with their start and end apart: 9 -> 4, of which waited for: 4 -> 1; matrix products, arithmetic and copies ran while one was open for 5% -> 20% of each run, Pallas kernels for 0% -> 53%
where the time goes in v1:
time: 135 us; the launch traced here: 134 us
  Pallas kernels  82.4 us (61%)
  between operations  14.3 us (11%)
  local copies, waits for them, and re-layouts  11.7 us (9%)
  matrix products  11.5 us (9%)
  other arithmetic  7.73 us (6%)
  waiting for transfers between devices  4.15 us (3%)
  starting transfers between devices  2.66 us (2%)
    pallas_call x2, Pallas kernels, gather_line(): pl.pallas_call(functools.partial(line_kernel, count), out_shape=jax.Shape...  32.4 us
    pallas_call x4, Pallas kernels, swap(): pl.pallas_call(functools.partial(swap_kernel, count, split), out_shape=[j...  25.2 us
    pallas_call x1, Pallas kernels, first_grad(): pl.pallas_call(functools.partial(first_kernel, high, wide), out_shape=jax...  20.2 us
    conv_general_dilated x4, matrix products, conv_plain(): lax.conv_general_dilated(field[None], kernel, strides, pads, lhs_dilation...  11.5 us
    pallas_call x1, Pallas kernels, second_grad(): pl.pallas_call(functools.partial(second_kernel, high, wide), out_shape=ja...  4.61 us
    ppermute x2, waiting for transfers between devices, shifted(): return lax.ppermute(shard, 'sp', pairs)  4.11 us
  transfers between devices with their start and end apart: 4, of which 1 were waited for; matrix products, arithmetic and copies ran while one was open for 20% of the time, Pallas kernels for 53%

profile of v1, /device:TPU:0, one launch (start us, length us, event | category | flops | bytes accessed | tf_op | source)
XLA Modules:
  0.0 134.4 jit_solution(13054669814633183963)
XLA Ops:
  7.2 0.0 copy-start
  7.2 0.0 all-gather.3.cloned.1.call-start
  7.2 1.4 %copy_bitcast_fusion.3.refs_1_ = bf16[2,1,4,4,128]{4,3,2,1,0:T(4,128)(2,1)} fusion(bf16[1,4,4,256]{3,2,1,0:T(4,128)(2,1)} %param.7), kind=kLoop, calls=%fused_computation.30 | loop fusion | bytes 16384 | tf_op jit(solution)/shard_map/transpose | solution.py:271
  8.6 6.8 %shard_map.75 = (bf16[2,2,8,8,256]{4,3,2,1,0:T(8,128)(2,1)}, bf16[2,1,4,4,128]{4,3,2,1,0:T(4,128)(2,1)}) custom-call(bf16[2,8,8,256]{3,2,1,0:T(8,128)(2,1)} %refs_0_.1, bf16[2,1,4,4,128]{4,3,2,1,0:T(4,128)(2,1)} %copy_bitcast_fusion.3.refs_1_), custom_call_target="tpu_custom_call" | custom-call | tf_op jit(solution)/shard_map/pallas_call | solution.py:122
  15.5 1.6 %copy.36 = bf16[2,2,8,8,256]{4,3,2,1,0:T(8,128)(2,1)} copy(bf16[2,2,8,8,256]{4,3,2,0,1:T(8,128)(2,1)} %bitcast.81) | data formatting | bytes 262144 | tf_op jit(solution)/shard_map/transpose | solution.py:280
  17.0 0.0 all-gather.3.cloned.1.call-update
  17.1 0.0 all-gather.5.cloned.1.call-start
  17.1 1.3 collective-permute-start
  18.4 0.8 slice.21
  19.3 1.3 collective-permute-start.1
  20.6 4.1 %collective-permute-done.1 = bf16[1,16,8,256]{3,2,1,0:T(8,128)(2,1)S(1)} collective-permute-done((bf16[1,16,8,256]{3,2,1,0:T(8,128)(2,1)S(1)}, bf16[1,16,8,256]{3,2,1,0:T(8,128)(2,1)S(1)}, u32[]{:S(2)}, u32[]{:S(2)}) %collective-permute-start.1) | collective-permute-done | bytes 65568 | tf_op jit(solution)/shard_map/ppermute | solution.py:236
  24.7 0.0 collective-permute-done
  24.7 0.9 maximum_bitcast_fusion
  25.6 0.0 copy-done
  25.7 4.1 %fusion = f32[1,3,16,8,128]{4,0,3,2,1:T(1,128)S(1)} fusion(bf16[128,3,3,3,256]{4,0,3,2,1:T(8,128)(2,1)S(1)} %copy-done, bf16[1,5,16,8,256]{4,3,2,1,0:T(8,128)(2,1)S(1)} %maximum_bitcast_fusion), kind=kOutput, calls=%fused_computation.1 | convolution fusion | flops 596901888 | bytes 2293760 | tf_op jit(solution)/shard_map/conv_general_dilated | solution.py:240
  29.8 0.7 select_convert_fusion.refs_0_
  30.5 6.2 %shard_map.76 = bf16[2,3,16,8,128]{4,3,2,1,0:T(8,128)(2,1)} custom-call(bf16[3,16,8,128]{3,2,1,0:T(8,128)(2,1)} %select_convert_fusion.refs_0_), custom_call_target="tpu_custom_call" | custom-call | tf_op jit(solution)/shard_map/pallas_call | solution.py:122
  36.7 0.0 copy-start.1
  36.7 1.0 slice.23
  37.7 0.1 copy.47
  37.8 0.1 reshape.126
  37.9 0.1 copy.48
  38.0 0.7 reshape.127
  38.7 0.0 all-gather.5.cloned.1.call-update
  38.7 0.5 iota_compare_fusion
  39.2 0.7 slice.22
  39.9 0.0 copy-done.1
  39.9 0.0 copy-start.4
  39.9 2.4 %fusion.2 = f32[1,1,8,4,128]{4,0,3,2,1:T(1,128)S(1)} fusion(bf16[128,3,3,3,256]{4,0,3,2,1:T(8,128)(2,1)} %param.6, bf16[1,3,16,8,256]{4,3,2,1,0:T(8,128)(2,1)S(1)} %copy_bitcast_fusion.1), kind=kOutput, calls=%fused_computation.3 | convolution fusion | flops 49741824 | bytes 1982464 | tf_op jit(solution)/shard_map/conv_general_dilated | solution.py:240
  42.3 0.0 copy-start.2
  42.3 0.6 copy-done.2
  42.9 0.0 copy-done.4
  42.9 0.6 fusion.13.own
  43.6 14.9 %shard_map.77 = bf16[16,32,128]{2,1,0:T(8,128)(2,1)} custom-call(bf16[32,128]{1,0:T(8,128)(2,1)} %fusion.13.own), custom_call_target="tpu_custom_call" | custom-call | tf_op jit(solution)/shard_map/pallas_call | solution.py:77
  58.5 0.9 copy.40
  59.5 0.0 copy-start.3
  59.5 2.6 %fusion.11 = f32[1,2,16,8,256]{4,0,3,2,1:T(1,128)S(1)} fusion(bf16[128,3,3,3,256]{4,0,3,2,1:T(8,128)(2,1)} %param.6, bf16[1,2,8,4,128]{4,2,3,1,0:T(8,128)(2,1)S(1)} %fusion.14), kind=kOutput, calls=%fused_computation.23 | convolution fusion | flops 49741824 | bytes 2048000 | tf_op jit(solution)/shard_map/conv_general_dilated | solution.py:240
  62.1 0.0 copy-done.3
  62.1 0.6 divide_multiply_fusion.refs_1_
  62.7 0.7 fusion.6.refs_0_
  63.4 6.2 %shard_map.78 = (bf16[2,2,16,8,128]{4,3,2,1,0:T(8,128)(2,1)}, f32[2,1,4,4,128]{4,3,2,1,0:T(4,128)}) custom-call(bf16[2,2,16,8,128]{4,3,2,1,0:T(8,128)(2,1)} %fusion.6.refs_0_, f32[2,1,4,4,128]{4,3,2,1,0:T(4,128)} %divide_multiply_fusion.refs_1_), custom_call_target="tpu_custom_call" | custom-call | tf_op jit(solution)/shard_map/pallas_call | solution.py:122
  69.6 1.0 select_reduce_fusion.1
  70.6 1.6 %fusion.9.own = bf16[2,128,128]{2,1,0:T(8,128)(2,1)} fusion(f32[2,16,8,128]{3,2,1,0:T(8,128)S(1)} %select_reduce_fusion.1, f32[2,128,128]{2,1,0:T(8,128)} %bitcast.80, f32[2,16,8,2,128]{4,2,3,1,0:T(8,128)S(1)} %bitcast.76, s32[]{:T(128)S(6)} %select_n.27), kind=kLoop, calls=%fused_computation.21 | loop fusion | flops 327680 | bytes 458756 | tf_op jit(solution)/shard_map/convert_element_type | solution.py:330
  72.2 17.5 %shard_map.79 = bf16[16,2,128,128]{3,2,1,0:T(8,128)(2,1)} custom-call(bf16[2,128,128]{2,1,0:T(8,128)(2,1)} %fusion.9.own), custom_call_target="tpu_custom_call" | custom-call | tf_op jit(solution)/shard_map/pallas_call | solution.py:77
  89.7 0.9 fusion.10
  90.6 2.4 %fusion.4 = f32[1,2,16,8,256]{4,0,3,2,1:T(1,128)S(1)} fusion(bf16[128,3,3,3,256]{4,0,3,2,1:T(8,128)(2,1)S(1)} %copy-done, bf16[1,4,16,8,128]{4,3,2,1,0:T(8,128)(2,1)S(1)} %fusion.10), kind=kOutput, calls=%fused_computation.7 | convolution fusion | flops 397934592 | bytes 2162688 | tf_op jit(solution)/shard_map/conv_general_dilated | solution.py:240
  93.1 0.7 copy.70
  93.7 6.0 %shard_map.80 = bf16[2,2,8,8,256]{4,3,2,1,0:T(8,128)(2,1)} custom-call(bf16[2,2,8,8,256]{4,3,2,1,0:T(8,128)(2,1)} %bitcast.78), custom_call_target="tpu_custom_call" | custom-call | tf_op jit(solution)/shard_map/pallas_call | solution.py:122
  99.7 1.0 select_reduce_fusion
  100.8 1.3 copy_bitcast_fusion.2
  102.1 0.7 bitcast_add_fusion
  102.8 0.0 all-gather.3.cloned.1.call-done
  102.8 20.2 %shard_map.81 = f32[9,384,256]{2,1,0:T(8,128)} custom-call(bf16[4096,256]{1,0:T(8,128)(2,1)} %bitcast.87, bf16[32,128,128]{2,1,0:T(8,128)(2,1)} %bitcast.66), custom_call_target="tpu_custom_call" | custom-call | flops 7247757312 | bytes 8388608 | tf_op jit(solution)/shard_map/pallas_call | solution.py:178
  122.9 0.0 all-gather.5.cloned.1.call-done.h_ref
  122.9 4.6 %shard_map.82 = f32[27,128,256]{2,1,0:T(8,128)} custom-call(bf16[16,8,32,256]{3,2,1,0:T(8,128)(2,1)} %all-gather.5.cloned.1.call-done.h_ref, bf16[512,128]{1,0:T(8,128)(2,1)} %bitcast.75), custom_call_target="tpu_custom_call" | custom-call | flops 905969664 | bytes 4194304 | tf_op jit(solution)/shard_map/pallas_call | solution.py:220
  (5 shorter events, 0.1 us)
Async XLA Ops:
  7.2 18.5 %copy-start = (bf16[128,3,3,3,256]{4,0,3,2,1:T(8,128)(2,1)S(1)}, bf16[128,3,3,3,256]{4,0,3,2,1:T(8,128)(2,1)}, u32[]{:S(2)}) copy-start(bf16[128,3,3,3,256]{4,0,3,2,1:T(8,128)(2,1)} %param.5) | copy-start | bytes 5308420
  7.2 95.6 %all-gather.3.cloned.1.call-start = ((), (), s32[]{:S(2)}) async-start(), calls=%async_computation | async-start | bytes 2228224 | tf_op jit(solution)/shard_map/all_gather | solution.py:307
  17.1 105.8 %all-gather.5.cloned.1.call-start = ((), (), s32[]{:S(2)}) async-start(), calls=%async_computation.1 | async-start | bytes 2228224 | tf_op jit(solution)/shard_map/all_gather | solution.py:316
  17.1 7.6 %collective-permute-start = (bf16[2,16,8,256]{3,2,1,0:T(8,128)(2,1)}, bf16[2,16,8,256]{3,2,1,0:T(8,128)(2,1)S(1)}, u32[]{:S(2)}, u32[]{:S(2)}) collective-permute-start(bf16[2,16,8,256]{3,2,1,0:T(8,128)(2,1)} %bitcast.72), channel_id=1, source_target_pairs={{0,2},{2,4},{4,6},{6,8},{8,10},{10,12},{12,14},{14,16},{16,18},{18... | collective-permute-start | bytes 393224 | tf_op jit(solution)/shard_map/ppermute | solution.py:236
  19.3 5.4 %collective-permute-start.1 = (bf16[1,16,8,256]{3,2,1,0:T(8,128)(2,1)S(1)}, bf16[1,16,8,256]{3,2,1,0:T(8,128)(2,1)S(1)}, u32[]{:S(2)}, u32[]{:S(2)}) collective-permute-start(bf16[1,16,8,256]{3,2,1,0:T(8,128)(2,1)S(1)} %bitcast.83), channel_id=1, source_target_pairs={{2,0},{4,2},{6,4},{8,6},{10,8},{12,10},{14,12},{16,14},{18,16},{20... | collective-permute-start | bytes 196616 | tf_op jit(solution)/shard_map/ppermute | solution.py:236
  36.7 3.2 %copy-start.1 = (bf16[2,3,16,8,128]{4,3,2,1,0:T(8,128)(2,1)S(1)}, bf16[2,3,16,8,128]{4,3,2,1,0:T(8,128)(2,1)}, u32[]{:S(2)}) copy-start(bf16[2,3,16,8,128]{4,3,2,1,0:T(8,128)(2,1)} %shard_map.76) | copy-start | bytes 589828
  39.9 3.0 %copy-start.4 = (bf16[2,1,4,4,128]{4,3,2,1,0:T(4,128)(2,1)S(1)}, bf16[2,1,4,4,128]{4,3,2,1,0:T(4,128)(2,1)}, u32[]{:S(2)}) copy-start(bf16[2,1,4,4,128]{4,3,2,1,0:T(4,128)(2,1)} %get-tuple-element.8) | copy-start | bytes 24580
  42.3 0.6 copy-start.2
  59.5 2.6 %copy-start.3 = (f32[1,1,8,4,128]{4,0,3,2,1:T(1,128)S(1)}, f32[1,1,8,4,128]{4,0,3,2,1:T(1,128)}, u32[]{:S(2)}) copy-start(f32[1,1,8,4,128]{4,0,3,2,1:T(1,128)} %copy-done.2) | copy-start | bytes 49156
Sparse Core Ops, SparseCore 0:
  17.2 43.0 all-gather.2
  62.4 43.5 all-gather.4
